TPU v7x, 256 devices: a whole 4x4x8 slice. The times are simulated.
256 devices in a mesh: prime: 8 (over z), row: 32 (over x, y, core).
Axes of the slice: x: 4, y: 4, z: 8, core: 2. Of those that a mesh axis runs over, the one named last changes fastest.
Arguments:
- tile_data: bfloat16 [8, 128, 17, 128, 128], P('prime', 'row'), may hold values from -0.125 to 0.125
- tile_slots: int32 [8, 128, 17], P('prime', 'row'), may hold values from 0 to 67, as said below
- requests: int32 [8, 32, 32, 2], P('prime'), may hold values from 0 to 3, as said below
- start_panel: bfloat16 [8, 16384, 128], P('prime', 'row'), may hold values from -6 to 6
- projectors: bfloat16 [8, 16384, 128], P('prime', 'row'), may hold values from -0.09375 to 0.09375
- combine_weights: float32 [8, 8], replicated, may hold values from -2 to 2
Outputs:
- projections_mixed: float32 [8, 6, 128, 128], P(None, None, 'row', 'prime')
- final_panel: bfloat16 [8, 16384, 128], P('prime', 'row')
Inputs may be any that keep to these rules, and one draw needn't show every extreme that they name: `tile_slots`: for each system and each device of row, the last slot of each of its 4 block rows is 64 plus the row's index among them, and the other slots of its rows together name each of 0 to 63 exactly once. `requests`: for each system, taking device and source device, the 2 entries are different.
All inputs are finite; a program needn't handle non-finite values.
Results may differ from a plain program's by a relative error of at most 0.02.
Values may be sent and summed in bfloat16 or wider, within the bound.
A program may use at most 64 MiB of HBM per device.

v0:
```python
import jax
import jax.numpy as jnp
from jax import lax
from jax.sharding import PartitionSpec as P

ITERS = 6


def select_blocks(blocks, positions):
    return blocks[positions]


def shards(tile_data, tile_slots, requests, start_panel, projectors, combine_weights):
    rank_count = lax.axis_size("row")
    my_index = lax.axis_index("row")
    local_primes, local_blocks, stored_tiles, tile_rows, tile_cols = tile_data.shape
    vec_width = start_panel.shape[2]
    fetched = requests.shape[3]
    exchanged = rank_count * fetched
    pick_rows = jax.vmap(select_blocks)
    own_wants = lax.dynamic_index_in_dim(requests, my_index, 1, keepdims=False)
    flat_wants = own_wants.reshape(local_primes, exchanged)
    inside = jnp.clip(tile_slots, 0, exchanged - 1).reshape(local_primes, -1)
    picked = jnp.take_along_axis(flat_wants, inside, axis=1).reshape(tile_slots.shape)
    columns = jnp.where(
        tile_slots < exchanged,
        tile_slots // fetched * local_blocks + picked,
        my_index * local_blocks + tile_slots - exchanged,
    )
    current_panel = start_panel
    projections = []
    for iteration in range(ITERS):
        partial_sum = jnp.einsum(
            "prw,prv->pwv", projectors, current_panel, preferred_element_type=jnp.float32
        )
        projections.append(
            lax.psum_scatter(
                partial_sum.astype(jnp.bfloat16), "row", scatter_dimension=1, tiled=True
            ).astype(jnp.float32)
        )
        gathered = lax.all_gather(current_panel, "row", axis=1, tiled=True)
        gathered = gathered.reshape(local_primes, rank_count * local_blocks, tile_rows, vec_width)
        needed_blocks = pick_rows(gathered, columns)
        product = jnp.einsum(
            "pikab,pikbw->piaw", tile_data, needed_blocks, preferred_element_type=jnp.float32
        )
        current_panel = product.astype(jnp.bfloat16).reshape(
            local_primes, local_blocks * tile_rows, vec_width
        )
    stacked = jnp.stack(projections, axis=1)
    regrouped = lax.all_to_all(stacked, "prime", split_axis=3, concat_axis=0, tiled=True)
    combined = jnp.einsum(
        "qp,pkab->qkab", combine_weights, regrouped, precision=lax.Precision.HIGHEST
    )
    return (combined, current_panel)


def solution(mesh):
    return jax.shard_map(
        shards,
        mesh=mesh,
        in_specs=(
            P("prime", "row", None, None, None),
            P("prime", "row", None),
            P("prime", None, None, None),
            P("prime", "row", None),
            P("prime", "row", None),
            P(),
        ),
        out_specs=(P(None, None, "row", "prime"), P("prime", "row", None)),
        check_vma=False,
    )
```

profile of v0, /device:TPU:1, one launch (start us, length us, event | category | flops | bytes accessed | tf_op | source)
XLA Modules:
  0.0 486.8 jit_solution(9364935634181028703)
XLA Ops:
  8.8 0.7 broadcast_clamp_fusion
  9.6 1.2 gather_fusion
  11.0 0.7 fusion.71
  11.8 54.1 %all-gather.7.cloned.1.call-done = bf16[1,16384,128]{2,1,0:T(8,128)(2,1)} async-done(((bf16[1,512,128]{2,1,0:T(8,128)(2,1)}), bf16[1,16384,128]{2,1,0:T(8,128)(2,1)}) %all-gather.7.cloned.1.call-update) | async-done | bytes 4194320 | tf_op jit(solution)/shard_map/all_gather | solution.py:41
  65.9 4.7 gather_fusion.1
  70.6 3.0 fusion.30
  73.7 50.6 %all-gather.9.cloned.1.call-done = bf16[1,16384,128]{2,1,0:T(8,128)(2,1)} async-done(((bf16[1,512,128]{2,1,0:T(8,128)(2,1)}), bf16[1,16384,128]{2,1,0:T(8,128)(2,1)}) %all-gather.9.cloned.1.call-update) | async-done | bytes 4194320 | tf_op jit(solution)/shard_map/all_gather | solution.py:41
  124.3 4.7 gather_fusion.2
  129.0 3.0 fusion.33
  132.1 50.6 %all-gather.11.cloned.1.call-done = bf16[1,16384,128]{2,1,0:T(8,128)(2,1)} async-done(((bf16[1,512,128]{2,1,0:T(8,128)(2,1)}), bf16[1,16384,128]{2,1,0:T(8,128)(2,1)}) %all-gather.11.cloned.1.call-update) | async-done | bytes 4194320 | tf_op jit(solution)/shard_map/all_gather | solution.py:41
  182.8 4.7 gather_fusion.3
  187.4 3.0 fusion.36
  190.5 50.6 %all-gather.13.cloned.1.call-done = bf16[1,16384,128]{2,1,0:T(8,128)(2,1)} async-done(((bf16[1,512,128]{2,1,0:T(8,128)(2,1)}), bf16[1,16384,128]{2,1,0:T(8,128)(2,1)}) %all-gather.13.cloned.1.call-update) | async-done | bytes 4194320 | tf_op jit(solution)/shard_map/all_gather | solution.py:41
  241.2 4.7 gather_fusion.4
  245.9 3.1 fusion.39
  249.0 0.8 fusion.48
  250.1 0.7 copy.32
  251.1 0.7 copy.33
  252.0 0.7 copy.34
  252.7 1.1 fusion.52
  253.9 0.7 copy.35
  254.6 45.0 %all-gather.15.cloned.1.call-done = bf16[1,16384,128]{2,1,0:T(8,128)(2,1)} async-done(((bf16[1,512,128]{2,1,0:T(8,128)(2,1)}), bf16[1,16384,128]{2,1,0:T(8,128)(2,1)}) %all-gather.15.cloned.1.call-update) | async-done | bytes 4194320 | tf_op jit(solution)/shard_map/all_gather | solution.py:41
  299.6 4.7 gather_fusion.5
  304.3 2.4 fusion.42
  307.0 0.7 copy.36
  309.8 108.3 %all-reduce.9.cloned.1.call-done = (bf16[1,128,128]{2,1,0:T(8,128)(2,1)}, bf16[1,128,128]{2,1,0:T(8,128)(2,1)}, bf16[1,128,128]{2,1,0:T(8,128)(2,1)}, bf16[1,128...) async-done(((bf16[1,128,128]{2,1,0:T(8,128)(2,1)}, bf16[1,128,128]{2,1,0:T(8,128)(2,1)}, bf16[1,128,128]{2,1,0:T(8,128)(2,1)}, ...) | async-done | bytes 196624
  420.1 0.7 constant_dynamic-update-slice_fusion.2
  421.5 0.7 constant_dynamic-update-slice_fusion
  422.6 13.1 %all_to_all.18 = f32[8,1,384]{2,1,0:T(1,128)S(1)} all-to-all(f32[8,1,384]{2,1,0:T(1,128)S(1)} %reshape.336), channel_id=1, replica_groups=mesh['prime'=8,'row'=32] {'prime'}, dimensions={0} | all-to-all | bytes 24576 | tf_op jit(solution)/shard_map/all_to_all | solution.py:51
  438.5 33.7 %all-gather.17.cloned.1.call-done = bf16[1,16384,128]{2,1,0:T(8,128)(2,1)} async-done(((bf16[1,512,128]{2,1,0:T(8,128)(2,1)}), bf16[1,16384,128]{2,1,0:T(8,128)(2,1)}) %all-gather.17.cloned.1.call-update) | async-done | bytes 4194320 | tf_op jit(solution)/shard_map/all_gather | solution.py:41
  472.2 4.7 gather_fusion.6
  476.9 3.0 fusion.45
  (59 shorter events, 10.4 us)
Async XLA Ops:
  7.2 63.5 %copy-start = (bf16[1,4,17,128,128]{4,3,2,1,0:T(8,128)(2,1)S(1)}, bf16[1,4,17,128,128]{4,3,2,1,0:T(8,128)(2,1)}, u32[]{:S(2)}) copy-start(bf16[1,4,17,128,128]{4,3,2,1,0:T(8,128)(2,1)} %param.6) | copy-start | bytes 6684676
  7.2 58.7 %all-gather.7.cloned.1.call-start = ((), (), s32[]{:S(2)}) async-start(), calls=%async_computation.1 | async-start | bytes 4325376 | tf_op jit(solution)/shard_map/all_gather | solution.py:41
  7.9 116.4 %all-gather.9.cloned.1.call-start = ((), (), s32[]{:S(2)}) async-start(), calls=%async_computation.2 | async-start | bytes 4325376 | tf_op jit(solution)/shard_map/all_gather | solution.py:41
  73.7 109.1 %all-gather.11.cloned.1.call-start = ((), (), s32[]{:S(2)}) async-start(), calls=%async_computation.3 | async-start | bytes 4325376 | tf_op jit(solution)/shard_map/all_gather | solution.py:41
  132.1 109.1 %all-gather.13.cloned.1.call-start = ((), (), s32[]{:S(2)}) async-start(), calls=%async_computation.4 | async-start | bytes 4325376 | tf_op jit(solution)/shard_map/all_gather | solution.py:41
  190.5 109.2 %all-gather.15.cloned.1.call-start = ((), (), s32[]{:S(2)}) async-start(), calls=%async_computation.5 | async-start | bytes 4325376 | tf_op jit(solution)/shard_map/all_gather | solution.py:41
  245.8 3.2 copy-start.1
  245.8 3.2 copy-start.6
  245.8 4.1 copy-start.3
  245.8 5.0 %copy-start.4 = (bf16[4,128,128]{1,2,0:T(8,128)(2,1)S(1)}, bf16[4,128,128]{1,2,0:T(8,128)(2,1)}, u32[]{:S(2)}) copy-start(bf16[4,128,128]{1,2,0:T(8,128)(2,1)} %fusion.33) | copy-start | bytes 393220
  245.8 6.0 %copy-start.5 = (bf16[4,128,128]{1,2,0:T(8,128)(2,1)S(1)}, bf16[4,128,128]{1,2,0:T(8,128)(2,1)}, u32[]{:S(2)}) copy-start(bf16[4,128,128]{1,2,0:T(8,128)(2,1)} %fusion.36) | copy-start | bytes 393220
  249.0 169.1 %all-reduce.9.cloned.1.call-start = ((), (), s32[]{:S(2)}) async-start(), calls=%async_computation.7 | async-start | bytes 393216
  304.3 4.2 copy-start.8
  304.3 133.3 %copy-start.7 = (f32[8,8]{1,0:T(8,128)S(1)}, f32[8,8]{1,0:T(8,128)}, u32[]{:S(2)}) copy-start(f32[8,8]{1,0:T(8,128)} %param.11) | copy-start | bytes 772
  306.7 1.1 copy-start.2
  307.7 164.5 %all-gather.17.cloned.1.call-start = ((), (), s32[]{:S(2)}) async-start(), calls=%async_computation.6 | async-start | bytes 4325376 | tf_op jit(solution)/shard_map/all_gather | solution.py:41
Sparse Core Ops, SparseCore 0:
  10.6 55.2 all-gather.6
  73.8 50.5 all-gather.8
  132.2 50.5 all-gather.10
  190.6 50.5 all-gather.12
  249.1 50.5 all-gather.14
  307.9 110.1 all-reduce.8
  421.5 50.6 all-gather.16
where the time goes:
time: 488 us; the launch traced here: 487 us
  waiting for transfers between devices  394 us (81%)
  local copies, waits for them, and re-layouts  41.2 us (8%)
  matrix products  20.6 us (4%)
  between operations  14.9 us (3%)
  blocking collectives  13.1 us (3%)
    all_gather x6, waiting for transfers between devices, shards(): gathered = lax.all_gather(current_panel, 'row', axis=1, tiled=True)  285 us
    unnamed x8, waiting for transfers between devices  110 us
    gather x8, local copies, waits for them, and re-layouts, select_blocks(): return blocks[positions]  28.3 us
    dot_general x6, matrix products, shards(): jnp.einsum('pikab,pikbw->piaw', tile_data, needed_blocks, preferred_eleme...  17.5 us
    all_to_all x1, blocking collectives, shards(): lax.all_to_all(stacked, 'prime', split_axis=3, concat_axis=0, tiled=True)  13.1 us
  transfers between devices with their start and end apart: 7, of which 7 were waited for; matrix products, arithmetic and copies ran while one was open for 4% of the time, Pallas kernels for 0%

commit v1 on v0

--- a/solution.py
+++ b/solution.py
@@ -4,6 +4,13 @@
 from jax.sharding import PartitionSpec as P
 
 ITERS = 6
+
+
+def exchange_gather(x, axis, d):
+    count = lax.axis_size(axis)
+    pieces = jnp.stack([x for _ in range(count)])
+    pieces = lax.all_to_all(pieces, axis, split_axis=0, concat_axis=0)
+    return jnp.concatenate(pieces, axis=d)
 
 
 def select_blocks(blocks, positions):
@@ -38,7 +45,7 @@
                 partial_sum.astype(jnp.bfloat16), "row", scatter_dimension=1, tiled=True
             ).astype(jnp.float32)
         )
-        gathered = lax.all_gather(current_panel, "row", axis=1, tiled=True)
+        gathered = exchange_gather(current_panel, "row", 1)
         gathered = gathered.reshape(local_primes, rank_count * local_blocks, tile_rows, vec_width)
         needed_blocks = pick_rows(gathered, columns)
         product = jnp.einsum(

time: 488 us -> 548 us (1.12)
  blocking collectives: 13.1 us -> 180 us
  waiting for transfers between devices: 394 us -> 259 us
  starting transfers between devices: 0.29 us -> 20.8 us
  local copies, waits for them, and re-layouts: 41.2 us -> 53.7 us
    all_gather x6 -> x0, waiting for transfers between devices: 285 us -> none  [shards(): gathered = lax.all_gather(current_panel, 'row', axis=1, tiled=True)]
    all_to_all x0 -> x3, blocking collectives: none -> 167 us  [exchange_gather(): pieces = lax.all_to_all(pieces, axis, split_axis=0, concat_axis=0)]
    all_to_all x0 -> x3, waiting for transfers between devices: none -> 147 us  [exchange_gather(): pieces = lax.all_to_all(pieces, axis, split_axis=0, concat_axis=0)]
    all_to_all x0 -> x3, starting transfers between devices: none -> 20.5 us  [exchange_gather(): pieces = lax.all_to_all(pieces, axis, split_axis=0, concat_axis=0)]
    another operation x0 -> x6, local copies, waits for them, and re-layouts: none -> 12.6 us  [exchange_gather(): pieces = jnp.stack([x for _ in range(count)])]
    unnamed x8 -> x2, waiting for transfers between devices: 110 us -> 112 us
  transfers between devices with their start and end apart: 7 -> 4, of which waited for: 7 -> 4; matrix products, arithmetic and copies ran while one was open for 4% -> 2% of each run, Pallas kernels for 0% -> 0%
where the time goes in v1:
time: 548 us; the launch traced here: 546 us
  waiting for transfers between devices  259 us (47%)
  blocking collectives  180 us (33%)
  local copies, waits for them, and re-layouts  53.7 us (10%)
  starting transfers between devices  20.8 us (4%)
  matrix products  17 us (3%)
  between operations  15 us (3%)
    all_to_all x3, blocking collectives, exchange_gather(): pieces = lax.all_to_all(pieces, axis, split_axis=0, concat_axis=0)  167 us
    all_to_all x3, waiting for transfers between devices, exchange_gather(): pieces = lax.all_to_all(pieces, axis, split_axis=0, concat_axis=0)  147 us
    unnamed x2, waiting for transfers between devices  112 us
    gather x8, local copies, waits for them, and re-layouts, select_blocks(): return blocks[positions]  28.3 us
    all_to_all x3, starting transfers between devices, exchange_gather(): pieces = lax.all_to_all(pieces, axis, split_axis=0, concat_axis=0)  20.5 us
    dot_general x6, matrix products, shards(): jnp.einsum('pikab,pikbw->piaw', tile_data, needed_blocks, preferred_eleme...  14.8 us
    all_to_all x1, blocking collectives, shards(): lax.all_to_all(stacked, 'prime', split_axis=3, concat_axis=0, tiled=True)  13.1 us
    another operation x6, local copies, waits for them, and re-layouts, exchange_gather(): pieces = jnp.stack([x for _ in range(count)])  12.6 us
  transfers between devices with their start and end apart: 4, of which 4 were waited for; matrix products, arithmetic and copies ran while one was open for 2% of the time, Pallas kernels for 0%

profile of v1, /device:TPU:1, one launch (start us, length us, event | category | flops | bytes accessed | tf_op | source)
XLA Modules:
  0.0 545.8 jit_solution(7073562340643803525)
XLA Ops:
  7.2 4.0 stack.36
  11.1 8.8 %all-to-all-start = ((bf16[32,1,512,128]{3,2,1,0:T(8,128)(2,1)}), bf16[32,1,512,128]{3,2,1,0:T(8,128)(2,1)}, u32[]{:S(2)}, u32[]{:S(2)}) async-start(bf16[32,1,512,128]{3,2,1,0:T(8,128)(2,1)} %stack.36), calls=%async_computation | async-start | bytes 8388608 | tf_op jit(solution)/shard_map/all_to_all | solution.py:12
  20.9 1.2 gather_fusion
  22.4 49.8 %all-to-all-done = bf16[32,1,512,128]{3,2,1,0:T(8,128)(2,1)} async-done(((bf16[32,1,512,128]{3,2,1,0:T(8,128)(2,1)}), bf16[32,1,512,128]{3,2,1,0:T(8,128)(2,1)}, u32[]{:S(2)}, u32[]{:S(2)}) %all-to-all-start) | async-done | bytes 4194336 | tf_op jit(solution)/shard_map/all_to_all | solution.py:12
  72.1 4.7 gather_fusion.1
  76.8 2.4 fusion.30
  79.2 0.9 stack.38
  80.2 57.6 %all_to_all.48 = bf16[32,1,512,128]{3,2,1,0:T(8,128)(2,1)} all-to-all(bf16[32,1,512,128]{3,2,1,0:T(8,128)(2,1)S(1)} %stack.38), channel_id=1, replica_groups=mesh['prime'=8,'row'=32] {'row'}, dimensions={0} | all-to-all | bytes 8388608 | tf_op jit(solution)/shard_map/all_to_all | solution.py:12
  137.8 4.7 gather_fusion.2
  142.5 2.4 fusion.33
  144.9 0.9 stack.40
  145.8 54.5 %all_to_all.49 = bf16[32,1,512,128]{3,2,1,0:T(8,128)(2,1)} all-to-all(bf16[32,1,512,128]{3,2,1,0:T(8,128)(2,1)S(1)} %stack.40), channel_id=1, replica_groups=mesh['prime'=8,'row'=32] {'row'}, dimensions={0} | all-to-all | bytes 8388608 | tf_op jit(solution)/shard_map/all_to_all | solution.py:12
  200.3 4.7 gather_fusion.3
  205.0 2.4 fusion.36
  207.3 0.9 stack.42
  208.3 54.5 %all_to_all.50 = bf16[32,1,512,128]{3,2,1,0:T(8,128)(2,1)} all-to-all(bf16[32,1,512,128]{3,2,1,0:T(8,128)(2,1)S(1)} %stack.42), channel_id=1, replica_groups=mesh['prime'=8,'row'=32] {'row'}, dimensions={0} | all-to-all | bytes 8388608 | tf_op jit(solution)/shard_map/all_to_all | solution.py:12
  262.8 4.7 gather_fusion.4
  267.5 2.4 fusion.39
  269.8 2.9 stack.44
  272.7 4.8 all-to-all-start.4
  277.8 0.8 fusion.48
  278.9 0.7 copy.32
  282.4 47.3 %all-to-all-done.4 = bf16[32,1,512,128]{3,2,1,0:T(8,128)(2,1)} async-done(((bf16[32,1,512,128]{3,2,1,0:T(8,128)(2,1)}), bf16[32,1,512,128]{3,2,1,0:T(8,128)(2,1)}, u32[]{:S(2)}, u32[]{:S(2)}) %all-to-all-start.4) | async-done | bytes 4194336 | tf_op jit(solution)/shard_map/all_to_all | solution.py:12
  329.7 4.7 gather_fusion.5
  334.4 2.4 fusion.42
  339.1 112.2 %all-reduce.9.cloned.1.call-done = (bf16[1,128,128]{2,1,0:T(8,128)(2,1)}, bf16[1,128,128]{2,1,0:T(8,128)(2,1)}, bf16[1,128,128]{2,1,0:T(8,128)(2,1)}, bf16[1,128...) async-done(((bf16[1,128,128]{2,1,0:T(8,128)(2,1)}, bf16[1,128,128]{2,1,0:T(8,128)(2,1)}, bf16[1,128,128]{2,1,0:T(8,128)(2,1)}, ...) | async-done | bytes 196624
  455.9 13.1 %all_to_all.51 = f32[8,1,384]{2,1,0:T(1,128)S(1)} all-to-all(f32[8,1,384]{2,1,0:T(1,128)S(1)} %reshape.325), channel_id=1, replica_groups=mesh['prime'=8,'row'=32] {'prime'}, dimensions={0} | all-to-all | bytes 24576 | tf_op jit(solution)/shard_map/all_to_all | solution.py:58
  469.0 2.9 stack.93
  472.0 7.0 %all-to-all-start.6 = ((bf16[32,1,512,128]{3,2,1,0:T(8,128)(2,1)}), bf16[32,1,512,128]{3,2,1,0:T(8,128)(2,1)}, u32[]{:S(2)}, u32[]{:S(2)}) async-start(bf16[32,1,512,128]{3,2,1,0:T(8,128)(2,1)} %stack.93), calls=%async_computation.6 | async-start | bytes 8388608 | tf_op jit(solution)/shard_map/all_to_all | solution.py:12
  481.7 49.5 %all-to-all-done.6 = bf16[32,1,512,128]{3,2,1,0:T(8,128)(2,1)} async-done(((bf16[32,1,512,128]{3,2,1,0:T(8,128)(2,1)}), bf16[32,1,512,128]{3,2,1,0:T(8,128)(2,1)}, u32[]{:S(2)}, u32[]{:S(2)}) %all-to-all-start.6) | async-done | bytes 4194336 | tf_op jit(solution)/shard_map/all_to_all | solution.py:12
  531.2 4.7 gather_fusion.6
  535.9 3.0 fusion.45
  (50 shorter events, 13.3 us)
Async XLA Ops:
  7.2 69.7 %copy-start = (bf16[1,4,17,128,128]{4,3,2,1,0:T(8,128)(2,1)S(1)}, bf16[1,4,17,128,128]{4,3,2,1,0:T(8,128)(2,1)}, u32[]{:S(2)}) copy-start(bf16[1,4,17,128,128]{4,3,2,1,0:T(8,128)(2,1)} %param.6) | copy-start | bytes 6684676
  11.1 9.7 %copy-start.3 = (s32[1,4,17]{2,1,0:T(4,128)S(1)}, s32[1,4,17]{2,1,0:T(4,128)}, u32[]{:S(2)}) copy-start(s32[1,4,17]{2,1,0:T(4,128)} %param.7) | copy-start | bytes 820
  11.1 61.0 %all-to-all-start = ((bf16[32,1,512,128]{3,2,1,0:T(8,128)(2,1)}), bf16[32,1,512,128]{3,2,1,0:T(8,128)(2,1)}, u32[]{:S(2)}, u32[]{:S(2)}) async-start(bf16[32,1,512,128]{3,2,1,0:T(8,128)(2,1)} %stack.36), calls=%async_computation | async-start | bytes 8388608 | tf_op jit(solution)/shard_map/all_to_all | solution.py:12
  272.7 5.0 copy-start.1
  272.7 5.0 copy-start.2
  272.7 57.0 %all-to-all-start.4 = ((bf16[32,1,512,128]{3,2,1,0:T(8,128)(2,1)}), bf16[32,1,512,128]{3,2,1,0:T(8,128)(2,1)}, u32[]{:S(2)}, u32[]{:S(2)}) async-start(bf16[32,1,512,128]{3,2,1,0:T(8,128)(2,1)} %stack.44), calls=%async_computation.4 | async-start | bytes 8388608 | tf_op jit(solution)/shard_map/all_to_all | solution.py:12
  277.5 173.8 %all-reduce.9.cloned.1.call-start = ((), (), s32[]{:S(2)}) async-start(), calls=%async_computation.7 | async-start | bytes 393216
  334.4 3.4 copy-start.5
  472.0 8.8 %copy-start.4 = (f32[8,8]{1,0:T(8,128)S(1)}, f32[8,8]{1,0:T(8,128)}, u32[]{:S(2)}) copy-start(f32[8,8]{1,0:T(8,128)} %param.11) | copy-start | bytes 772
  472.0 59.3 %all-to-all-start.6 = ((bf16[32,1,512,128]{3,2,1,0:T(8,128)(2,1)}), bf16[32,1,512,128]{3,2,1,0:T(8,128)(2,1)}, u32[]{:S(2)}, u32[]{:S(2)}) async-start(bf16[32,1,512,128]{3,2,1,0:T(8,128)(2,1)} %stack.93), calls=%async_computation.6 | async-start | bytes 8388608 | tf_op jit(solution)/shard_map/all_to_all | solution.py:12
Sparse Core Ops, SparseCore 0:
  337.9 113.4 all-reduce.8
